TPU v7x, 128 devices: a whole 4x4x4 slice. The times are simulated.
128 devices in a mesh: freq: 8 (over x, y_lo), tm: 16 (over z, y_hi, core).
Axes of the slice: x: 4, y: 4 (y_hi: 2, y_lo: 2; y = y_hi * 2 + y_lo), z: 4, core: 2. Of those that a mesh axis runs over, the one named last changes fastest.
Arguments:
- voltages: bfloat16 [2048, 530432], P(('tm', 'freq')), may hold values from -128 to 127, as said below
- fir_taps: float32 [4, 2048], replicated, may hold values from -3 to 3
Outputs:
- coherence: bfloat16 [2, 64, 2048, 2048], P(None, 'freq', 'tm')
Inputs may be any that keep to these rules, and one draw needn't show every extreme that they name: `voltages`: every sample is a whole number.
All inputs are finite; a program needn't handle non-finite values.
Results may differ from a plain program's by a relative error of at most 0.0073.
Values may be sent and summed in bfloat16 or wider, within the bound.
A program may use at most 192 MiB of HBM per device.

v0:
```python
import math
import jax
import jax.numpy as jnp
from jax import lax
from jax.sharding import PartitionSpec as P

P_SIZE = 2048
TAPS = 4
FIRST_BIN = 512
CH_DEV = 8
S = 256


def dft_table(channels):
    points = jnp.arange(P_SIZE, dtype=jnp.int32)
    bins = FIRST_BIN + jnp.arange(channels, dtype=jnp.int32)
    phase = points[:, None] * bins[None, :] % P_SIZE
    angle = 2.0 * math.pi / P_SIZE * phase.astype(jnp.float32)
    twiddle = jnp.stack([jnp.cos(angle), -jnp.sin(angle)], axis=2)
    return twiddle.reshape(P_SIZE, 2 * channels).astype(jnp.bfloat16)


def filter_frames(block, fir_taps):
    inputs_here = block.shape[0]
    samples = block.astype(jnp.float32).reshape(inputs_here, S + TAPS - 1, P_SIZE)
    frames = fir_taps[0] * samples[:, 0:S]
    for tap_index in range(1, TAPS):
        frames = frames + fir_taps[tap_index] * samples[:, tap_index : tap_index + S]
    return frames.astype(jnp.bfloat16).reshape(inputs_here * S, P_SIZE)


def correlate(own_spectra, column_block):
    slab = own_spectra.shape[0]
    rows_here = own_spectra.shape[2]
    width = column_block.shape[2]
    left_rows = own_spectra.reshape(slab, 2 * rows_here, S)
    right_rows = column_block.reshape(slab, 2 * width, S)
    products = lax.dot_general(
        left_rows, right_rows, (((2,), (2,)), ((0,), (0,))), preferred_element_type=jnp.float32
    )
    products = products.reshape(slab, 2, rows_here, 2, width)
    real_part = products[:, 0, :, 0] + products[:, 1, :, 1]
    imag_part = products[:, 1, :, 0] - products[:, 0, :, 1]
    return jnp.stack([real_part, imag_part])


def on_device(voltages, fir_taps):
    freq_count = lax.axis_size("freq")
    channels = CH_DEV * freq_count
    inputs_here = voltages.shape[0]
    frames = filter_frames(voltages, fir_taps)
    twiddle = dft_table(channels)
    spectra = lax.dot_general(
        twiddle, frames, (((0,), (1,)), ((), ())), preferred_element_type=jnp.float32
    )
    spectra = spectra.astype(jnp.bfloat16).reshape(channels, 2, inputs_here, S)
    own_spectra = lax.all_to_all(spectra, "freq", split_axis=0, concat_axis=2, tiled=True)
    all_spectra = lax.all_gather(own_spectra, "tm", axis=2, tiled=True)
    raw_sums = correlate(own_spectra, all_spectra)
    wide = own_spectra.astype(jnp.float32)
    powers = jnp.sum(wide * wide, axis=(1, 3)) / S + 1e-06
    powers_all = lax.all_gather(powers, "tm", axis=1, tiled=True)
    row_scale = lax.rsqrt(powers) / S
    column_scale = lax.rsqrt(powers_all)
    coherence = raw_sums * row_scale[None, :, :, None] * column_scale[None, :, None, :]
    return coherence.astype(jnp.bfloat16)


def solution(mesh):
    placed = (P(("tm", "freq"), None), P())
    return jax.shard_map(
        on_device,
        mesh=mesh,
        in_specs=placed,
        out_specs=P(None, "freq", "tm", None),
        check_vma=False,
    )
```

profile of v0, /device:TPU:1, one launch (start us, length us, event | category | flops | bytes accessed | tf_op | source)
XLA Modules:
  0.0 373.9 jit_solution(2463869961442593070)
XLA Ops:
  6.5 0.0 all-gather.2.cloned.1.call-start
  6.5 0.9 fusion.15
  7.5 2.5 cosine_convert_fusion
  9.9 0.1 pad_maximum_fusion
  10.0 0.5 copy.13
  10.5 0.2 convert_element_type.41
  10.8 25.4 %reshape.197 = f32[16,259,2048]{2,1,0:T(8,128)} reshape(bf16[16,530432]{1,0:T(8,128)(2,1)} %param.2) | data formatting | bytes 50921472 | tf_op jit(solution)/shard_map/reshape | solution.py:25
  36.1 49.4 %fusion.1 = bf16[16,256,2048]{2,1,0:T(8,128)(2,1)} fusion(f32[16,259,2048]{2,1,0:T(8,128)} %reshape.197, f32[2048]{0:T(1024)S(1)} %bitcast.36, f32[2048]{0:T(1024)S(1)} %bitcast.37, f32[2048]{0:T(1024)S(1)} %bitcast.35, f32[2048]{0:T(1024)S(1)} %bitcast.34), kind=kLoop, calls=%fused_computation.2 | loop fusion | flops 67108864 | bytes 151027712 | tf_op jit(solution)/shard_map/convert_element_type | solution.py:29
  85.5 11.4 %convolution_convert_fusion = bf16[128,4096]{1,0:T(8,128)(2,1)S(1)} fusion(bf16[2048,128]{0,1:T(8,128)(2,1)S(1)} %convert_element_type.41, bf16[4096,2048]{1,0:T(8,128)(2,1)} %bitcast.26), kind=kOutput, calls=%fused_computation.15 | convolution fusion | flops 2148007936 | bytes 18350080 | tf_op jit(solution)/shard_map/dot_general | solution.py:53
  96.9 0.2 copy.23
  97.2 20.0 %all_to_all.18 = bf16[64,2,16,256]{3,2,1,0:T(8,128)(2,1)S(1)} all-to-all(bf16[64,2,16,256]{3,2,1,0:T(8,128)(2,1)S(1)} %bitcast.33), channel_id=1, replica_groups=mesh['freq'=8,'tm'=16] {'freq'}, dimensions={0} | all-to-all | bytes 2097152 | tf_op jit(solution)/shard_map/all_to_all | solution.py:57
  117.1 1.1 copy.14
  118.2 0.0 all-gather.2.cloned.1.call-update
  118.3 0.3 multiply_reduce_fusion
  118.5 0.1 add.76
  118.6 27.9 %all_gather.7 = f32[8,2048]{1,0:T(8,128)S(1)} all-gather(f32[8,128]{1,0:T(8,128)S(1)} %add.76), channel_id=1, replica_groups=mesh['freq'=8,'tm'=16] {'tm'}, dimensions={1}, use_global_device_ids=true | all-gather | bytes 69632 | tf_op jit(solution)/shard_map/all_gather | solution.py:62
  146.5 83.9 %all-gather.2.cloned.1.call-done = bf16[8,2,2048,256]{3,2,1,0:T(8,128)(2,1)} async-done(((bf16[8,2,128,256]{3,2,1,0:T(8,128)(2,1)}), bf16[8,2,2048,256]{3,2,1,0:T(8,128)(2,1)}) %all-gather.2.cloned.1.call-update) | async-done | bytes 16777232 | tf_op jit(solution)/shard_map/all_gather | solution.py:58
  230.5 17.4 %fusion.16 = f32[8,256,4096]{2,1,0:T(8,128)} fusion(bf16[8,256,256]{2,1,0:T(8,128)(2,1)} %bitcast.29, bf16[8,4096,256]{2,1,0:T(8,128)(2,1)} %bitcast.27), kind=kOutput, calls=%fused_computation.34 | convolution fusion | flops 4294967296 | bytes 51380224 | tf_op jit(solution)/shard_map/dot_general | solution.py:38
  247.9 42.6 %reshape.195 = f32[8,2,128,2,2048]{4,3,2,1,0:T(2,128)} reshape(f32[8,256,4096]{2,1,0:T(8,128)} %fusion.16) | data formatting | bytes 67108864 | tf_op jit(solution)/shard_map/reshape | solution.py:41
  290.6 39.8 %fusion.14 = (f32[8,1,128,1,2048]{4,3,2,1,0:T(1,128)}, f32[8,1,128,1,2048]{4,3,2,1,0:T(1,128)}, f32[8,1,128,1,2048]{4,3,2,1,0:T(1,128)}, f32[8,1,128,1,2048]{4,3,2,1,0:T(1,128)}) fusion(f32[8,2,128,2,2048]{4,3,2,1,0:T(2,128)} %reshape.195), kind=kLoop, calls=%fused_computation.32 | loop fusion | bytes 67108864 | tf_op jit(solution)/shard_map/slice | solution.py:42
  330.4 26.8 %fusion.6 = (f32[1,8,128,2048]{3,2,1,0:T(8,128)}, f32[1,8,128,2048]{3,2,1,0:T(8,128)}) fusion(f32[8,1,128,1,2048]{4,3,2,1,0:T(1,128)} %get-tuple-element.8, f32[8,1,128,1,2048]{4,3,2,1,0:T(1,128)} %get-tuple-element.6, f32[8,1,128,1,2048]{4,3,2,1,0:T(1,128)} %get-tuple-element.7, f32[8,1,128,1,2048]{4,3,2,1,0:T(1,128)} %get-tuple-element.5), kind=kLoop, calls=%fused_computation.12 | loop fusion | flops 4194304 | bytes 50331648 | tf_op jit(solution)/shard_map/sub | solution.py:43
  357.2 9.9 %fusion.5 = bf16[2,8,128,2048]{3,2,1,0:T(8,128)(2,1)} fusion(f32[1,8,128,2048]{3,2,1,0:T(8,128)} %get-tuple-element.15, f32[1,8,128,2048]{3,2,1,0:T(8,128)} %get-tuple-element.16, f32[8,2048]{1,0:T(8,128)S(1)} %rsqrt.11, f32[8,128]{1,0:T(8,128)S(1)} %rsqrt_multiply_fusion), kind=kLoop, calls=%fused_computation.10 | loop fusion | flops 16777216 | bytes 25235456 | tf_op jit(solution)/shard_map/convert_element_type | solution.py:66
  (4 shorter events, 0.0 us)
Async XLA Ops:
  6.5 224.0 %all-gather.2.cloned.1.call-start = ((), (), s32[]{:S(2)}) async-start(), calls=%async_computation.1 | async-start | bytes 17825792 | tf_op jit(solution)/shard_map/all_gather | solution.py:58
Sparse Core Ops, SparseCore 0:
  118.4 112.0 all-gather.1
where the time goes:
time: 375 us; the launch traced here: 374 us
  local copies, waits for them, and re-layouts  111 us (30%)
  other arithmetic  88.9 us (24%)
  waiting for transfers between devices  84 us (22%)
  blocking collectives  47.9 us (13%)
  matrix products  28.8 us (8%)
  between operations  13.5 us (4%)
    all_gather x1, waiting for transfers between devices, on_device(): all_spectra = lax.all_gather(own_spectra, 'tm', axis=2, tiled=True)  83.9 us
    convert_element_type x1, other arithmetic, filter_frames(): return frames.astype(jnp.bfloat16).reshape(inputs_here * S, P_SIZE)  49.4 us
    reshape x1, local copies, waits for them, and re-layouts, correlate(): products = products.reshape(slab, 2, rows_here, 2, width)  42.6 us
    slice x1, local copies, waits for them, and re-layouts, correlate(): real_part = products[:, 0, :, 0] + products[:, 1, :, 1]  39.8 us
    all_gather x1, blocking collectives, on_device(): powers_all = lax.all_gather(powers, 'tm', axis=1, tiled=True)  27.9 us
    sub x1, other arithmetic, correlate(): imag_part = products[:, 1, :, 0] - products[:, 0, :, 1]  26.8 us
    reshape x1, local copies, waits for them, and re-layouts, filter_frames(): block.astype(jnp.float32).reshape(inputs_here, S + TAPS - 1, P_SIZE)  25.4 us
    all_to_all x1, blocking collectives, on_device(): lax.all_to_all(spectra, 'freq', split_axis=0, concat_axis=2, tiled=True)  20 us
  transfers between devices with their start and end apart: 1, of which 1 were waited for; matrix products, arithmetic and copies ran while one was open for 0% of the time, Pallas kernels for 0%

commit v1 on v0

--- a/solution.py
+++ b/solution.py
@@ -54,7 +54,10 @@
         twiddle, frames, (((0,), (1,)), ((), ())), preferred_element_type=jnp.float32
     )
     spectra = spectra.astype(jnp.bfloat16).reshape(channels, 2, inputs_here, S)
-    own_spectra = lax.all_to_all(spectra, "freq", split_axis=0, concat_axis=2, tiled=True)
+    own_spectra = jnp.concatenate(
+        lax.all_to_all(jnp.stack(jnp.split(spectra, lax.axis_size("freq"), axis=0)), "freq", 0, 0),
+        axis=2,
+    )
     all_spectra = lax.all_gather(own_spectra, "tm", axis=2, tiled=True)
     raw_sums = correlate(own_spectra, all_spectra)
     wide = own_spectra.astype(jnp.float32)

time: 375 us -> 375 us (level)
  no operation moved by 1% of the time
where the time goes in v1:
time: 375 us; the launch traced here: 374 us
  local copies, waits for them, and re-layouts  111 us (30%)
  other arithmetic  88.9 us (24%)
  waiting for transfers between devices  84 us (22%)
  blocking collectives  47.7 us (13%)
  matrix products  28.8 us (8%)
  between operations  13.6 us (4%)
    all_gather x1, waiting for transfers between devices, on_device(): all_spectra = lax.all_gather(own_spectra, 'tm', axis=2, tiled=True)  84 us
    convert_element_type x1, other arithmetic, filter_frames(): return frames.astype(jnp.bfloat16).reshape(inputs_here * S, P_SIZE)  49.4 us
    reshape x1, local copies, waits for them, and re-layouts, correlate(): products = products.reshape(slab, 2, rows_here, 2, width)  42.6 us
    slice x1, local copies, waits for them, and re-layouts, correlate(): real_part = products[:, 0, :, 0] + products[:, 1, :, 1]  39.8 us
    all_gather x1, blocking collectives, on_device(): powers_all = lax.all_gather(powers, 'tm', axis=1, tiled=True)  27.7 us
    sub x1, other arithmetic, correlate(): imag_part = products[:, 1, :, 0] - products[:, 0, :, 1]  26.8 us
    reshape x1, local copies, waits for them, and re-layouts, filter_frames(): block.astype(jnp.float32).reshape(inputs_here, S + TAPS - 1, P_SIZE)  25.3 us
    all_to_all x1, blocking collectives, on_device(): lax.all_to_all(jnp.stack(jnp.split(spectra, lax.axis_size('freq'), axis=0...  20 us
  transfers between devices with their start and end apart: 1, of which 1 were waited for; matrix products, arithmetic and copies ran while one was open for 0% of the time, Pallas kernels for 0%

profile of v1, /device:TPU:1, one launch (start us, length us, event | category | flops | bytes accessed | tf_op | source)
XLA Modules:
  0.0 374.0 jit_solution(15326560489870455154)
XLA Ops:
  6.5 0.0 all-gather.2.cloned.1.call-start
  6.5 0.9 fusion.16
  7.5 2.5 cosine_convert_fusion
  9.9 0.1 pad_maximum_fusion
  10.0 0.5 copy.25
  10.5 0.2 convert_element_type.41
  10.8 25.3 %reshape.213 = f32[16,259,2048]{2,1,0:T(8,128)} reshape(bf16[16,530432]{1,0:T(8,128)(2,1)} %param.2) | data formatting | bytes 50921472 | tf_op jit(solution)/shard_map/reshape | solution.py:25
  36.1 49.4 %fusion.1 = bf16[16,256,2048]{2,1,0:T(8,128)(2,1)} fusion(f32[16,259,2048]{2,1,0:T(8,128)} %reshape.213, f32[2048]{0:T(1024)S(1)} %bitcast.68, f32[2048]{0:T(1024)S(1)} %bitcast.69, f32[2048]{0:T(1024)S(1)} %bitcast.67, f32[2048]{0:T(1024)S(1)} %bitcast.66), kind=kLoop, calls=%fused_computation.2 | loop fusion | flops 67108864 | bytes 151027712 | tf_op jit(solution)/shard_map/convert_element_type | solution.py:29
  85.5 11.4 %convolution_convert_fusion = bf16[128,4096]{1,0:T(8,128)(2,1)S(1)} fusion(bf16[2048,128]{0,1:T(8,128)(2,1)S(1)} %convert_element_type.41, bf16[4096,2048]{1,0:T(8,128)(2,1)} %bitcast.46), kind=kOutput, calls=%fused_computation.15 | convolution fusion | flops 2148007936 | bytes 18350080 | tf_op jit(solution)/shard_map/dot_general | solution.py:53
  96.9 0.1 fusion.15
  97.4 20.0 %all_to_all.5 = bf16[8,8,2,16,256]{4,3,2,1,0:T(8,128)(2,1)S(1)} all-to-all(bf16[8,8,2,16,256]{4,3,2,1,0:T(8,128)(2,1)S(1)} %constant_dynamic-update-slice_fusion), channel_id=1, replica_groups=mesh['freq'=8,'tm'=16] {'freq'}, dimensions={0} | all-to-all | bytes 2097152 | tf_op jit(solution)/shard_map/all_to_all | solution.py:58
  117.4 1.1 copy.26
  118.5 0.0 all-gather.2.cloned.1.call-update
  118.5 0.3 multiply_reduce_fusion
  118.8 0.1 add.76
  118.8 27.7 %all_gather.7 = f32[8,2048]{1,0:T(8,128)S(1)} all-gather(f32[8,128]{1,0:T(8,128)S(1)} %add.76), channel_id=1, replica_groups=mesh['freq'=8,'tm'=16] {'tm'}, dimensions={1}, use_global_device_ids=true | all-gather | bytes 69632 | tf_op jit(solution)/shard_map/all_gather | solution.py:65
  146.6 84.0 %all-gather.2.cloned.1.call-done = bf16[8,2,2048,256]{3,2,1,0:T(8,128)(2,1)} async-done(((bf16[8,2,128,256]{3,2,1,0:T(8,128)(2,1)}), bf16[8,2,2048,256]{3,2,1,0:T(8,128)(2,1)}) %all-gather.2.cloned.1.call-update) | async-done | bytes 16777232 | tf_op jit(solution)/shard_map/all_gather | solution.py:61
  230.6 17.4 %fusion.17 = f32[8,256,4096]{2,1,0:T(8,128)} fusion(bf16[8,256,256]{2,1,0:T(8,128)(2,1)} %bitcast.49, bf16[8,4096,256]{2,1,0:T(8,128)(2,1)} %bitcast.47), kind=kOutput, calls=%fused_computation.43 | convolution fusion | flops 4294967296 | bytes 51380224 | tf_op jit(solution)/shard_map/dot_general | solution.py:38
  248.0 42.6 %reshape.211 = f32[8,2,128,2,2048]{4,3,2,1,0:T(2,128)} reshape(f32[8,256,4096]{2,1,0:T(8,128)} %fusion.17) | data formatting | bytes 67108864 | tf_op jit(solution)/shard_map/reshape | solution.py:41
  290.6 39.8 %fusion.14 = (f32[8,1,128,1,2048]{4,3,2,1,0:T(1,128)}, f32[8,1,128,1,2048]{4,3,2,1,0:T(1,128)}, f32[8,1,128,1,2048]{4,3,2,1,0:T(1,128)}, f32[8,1,128,1,2048]{4,3,2,1,0:T(1,128)}) fusion(f32[8,2,128,2,2048]{4,3,2,1,0:T(2,128)} %reshape.211), kind=kLoop, calls=%fused_computation.40 | loop fusion | bytes 67108864 | tf_op jit(solution)/shard_map/slice | solution.py:42
  330.4 26.8 %fusion.6 = (f32[1,8,128,2048]{3,2,1,0:T(8,128)}, f32[1,8,128,2048]{3,2,1,0:T(8,128)}) fusion(f32[8,1,128,1,2048]{4,3,2,1,0:T(1,128)} %get-tuple-element.8, f32[8,1,128,1,2048]{4,3,2,1,0:T(1,128)} %get-tuple-element.6, f32[8,1,128,1,2048]{4,3,2,1,0:T(1,128)} %get-tuple-element.7, f32[8,1,128,1,2048]{4,3,2,1,0:T(1,128)} %get-tuple-element.5), kind=kLoop, calls=%fused_computation.12 | loop fusion | flops 4194304 | bytes 50331648 | tf_op jit(solution)/shard_map/sub | solution.py:43
  357.2 9.9 %fusion.5 = bf16[2,8,128,2048]{3,2,1,0:T(8,128)(2,1)} fusion(f32[1,8,128,2048]{3,2,1,0:T(8,128)} %get-tuple-element.23, f32[1,8,128,2048]{3,2,1,0:T(8,128)} %get-tuple-element.24, f32[8,2048]{1,0:T(8,128)S(1)} %rsqrt.11, f32[8,128]{1,0:T(8,128)S(1)} %rsqrt_multiply_fusion), kind=kLoop, calls=%fused_computation.10 | loop fusion | flops 16777216 | bytes 25235456 | tf_op jit(solution)/shard_map/convert_element_type | solution.py:69
  (20 shorter events, 0.3 us)
Async XLA Ops:
  6.5 224.0 %all-gather.2.cloned.1.call-start = ((), (), s32[]{:S(2)}) async-start(), calls=%async_computation.1 | async-start | bytes 17825792 | tf_op jit(solution)/shard_map/all_gather | solution.py:61
Sparse Core Ops, SparseCore 0:
  118.6 111.9 all-gather.1
